TPU v7x, 256 devices: a whole 4x4x8 slice. The times are simulated.
256 devices in a mesh: dp: 4 (over y), expert: 64 (over z, x, core).
Axes of the slice: x: 4, y: 4, z: 8, core: 2. Of those that a mesh axis runs over, the one named last changes fastest.
Arguments:
- tokens: bfloat16 [8192, 3584], P('expert', 'dp'), may hold values from -6 to 6
- expert_ids: int32 [8192, 8], P('expert'), may hold values from 0 to 63, as said below
- replica_choice: int32 [8192, 8], P('expert'), may hold values from 0 to 1, as said below
- gate_weights: float32 [8192, 8], P('expert'), may hold values from 0.1 to 1
- placement: int32 [32, 2], replicated, may hold values from 0 to 63, as said below
- capacity: int32 [96], replicated, may hold values from 6 to 12, as said below
- w_gate: bfloat16 [64, 2, 3584, 1024], P('expert', None, 'dp'), as said below
- w_up: bfloat16 [64, 2, 3584, 1024], P('expert', None, 'dp'), as said below
- w_down: bfloat16 [64, 2, 1024, 3584], P('expert', None, None, 'dp'), as said below
Outputs:
- combined: bfloat16 [8192, 3584], P('expert', 'dp')
Inputs may be any that keep to these rules, and one draw needn't show every extreme that they name: `expert_ids`: each row names 8 different experts; in every aligned block of 128 rows some hot expert is named by at least 24 rows. `replica_choice`: 1 only where the slot's expert is hot; in every aligned block of 128 rows both replicas of some hot expert whose replicas have capacity 12 receive 12 or more slots. `placement`: column 0 holds 32 different expert numbers; column 1 holds 32 different expert-axis indices, none of them the own index of a hot expert. Entry e below 64 belongs to expert e's own replica, entry 64 + j to the copy of expert placement[j, 0]; both replicas of some hot expert have capacity 12. w_gate[placement[j, 1], 1] equals w_gate[placement[j, 0], 0]; entry [h, 1] is zero where index h hosts no copy. `w_up`: laid out as w_gate. `w_down`: laid out as w_gate.
All inputs are finite; a program needn't handle non-finite values.
Results may differ from a plain program's by a relative error of at most 0.0057.
Values may be sent and summed in bfloat16 or wider, within the bound.
A program may use at most 128 MiB of HBM per device.

v0:
```python
import functools

import jax
import jax.numpy as jnp
from jax import lax
from jax.experimental import pallas as pl
from jax.experimental.pallas import tpu as pltpu
from jax.sharding import PartitionSpec as P

MESH = pl.DeviceIdType.MESH
F32 = jnp.float32
BF16 = jnp.bfloat16
I32 = jnp.int32
LANES = 128
CODE = 64
ALIGN = 8

SIZES = dict(
    nz=8, nx=4, nc=2, cap=12,
    groups=((0,), (1, -1), (2, -2), (3, -3), (4,)),
    order=(0, 1, -2, 4, 3, -3, 2, -1),
    returns=((0, 1), (-2, 4), (3,), (-3,), (2,), (-1,)),
    early=(
        "d0 r10 r11 d1", "w a0 u0 r20", "s0 r21 d2 c0", "r30 a1 u1 r31", "d3 p0 s1 r40", "a2 u2 r41 d4", "c1 s2",
    ),
    begin=(3, 3, 2, 1, 0),
    before={3: "a4", 4: "a3"},
    after={5: "o0", 7: "o1 m0", 8: "o2 m1 R1", 9: "o3 m2 R2", 10: "o4 m3 L1", 11: "o5 L2"},
    late=("m4 R3 m5", "L3 R4"),
)


def room(cfg, blocks):
    return -(-blocks * (cfg["cap"] + cfg["cap"] // 2) // ALIGN) * ALIGN


def kernel(cfg, *refs):
    groups, order, returns = cfg["groups"], cfg["order"], cfg["returns"]
    ng, nr = len(groups), len(returns)
    refs = list(refs)

    def take(n):
        out = refs[:n]
        del refs[:n]
        return out

    tok_ref, ids_ref, rep_ref, gw_ref, place_ref, place_s, cap_ref, wg_hbm, wu_hbm, wd_hbm = take(10)
    (out_ref,) = take(1)
    wg, wu, wd, w_sem = take(4)
    tokg, codes, z_ssem, z_rsem = take(4)
    xs, xr = take(ng), take(ng)
    x_ssem, x_rsem, xc = take(3)
    part, r1s, r1r, r2s, r2r, hid, res = take(7)
    r1_ssem, r1_rsem, r2_ssem, r2_rsem, a1_ssem, a1_rsem, a2_ssem, a2_rsem = take(8)
    os_, or_ = take(nr), take(nr)
    o_ssem, o_rsem = take(2)
    acc, csend, crecv, c_ssem, c_rsem = take(5)
    assert not refs

    nz, nx, nc, cap = cfg["nz"], cfg["nx"], cfg["nc"], cfg["cap"]
    half = cap // 2
    each = cap + half
    experts = nz * nx * nc
    hot = place_ref.shape[1]
    top = ids_ref.shape[0]
    tb, cols = tok_ref.shape
    far = nz // 2
    slots = nx * nc
    ua, ub = slots * cap, slots * half
    ur = ua + ub
    units = nz
    flat = [b for g in groups for b in g]
    entry = {b: i for i, b in enumerate(flat)}
    place_of = {b: i for i, b in enumerate(order)}

    y = lax.axis_index("dp")
    e = lax.axis_index("expert")
    z = e // slots
    x = (e // nc) % nx
    c = e % nc

    def dev(yy, zz, xx, cc):
        return (yy, (zz * nx + xx) * nc + cc)

    right = dev(y, lax.rem(z + 1, nz), x, c)
    left = dev(y, lax.rem(z + nz - 1, nz), x, c)
    odd, high = y % 2, y // 2
    mate1 = dev(y + 1 - 2 * odd, z, x, c)
    mate2 = dev(3 - y, z, x, c)
    first_mate = (mate1, mate2)
    second_mate = (mate2, mate1)
    keep_half = ((odd + high) % 2, high)
    keep_quarter = (high, odd)

    def slot_dest(s):
        dx, dc = s // nc, s % nc
        return lax.rem(x + dx, nx), lax.rem(c + dc, nc)

    def slot_source(s):
        dx, dc = s // nc, s % nc
        return lax.rem(x + nx - dx, nx), lax.rem(c + nc - dc, nc)

    loads = [
        pltpu.make_async_copy(h.at[0], v, w_sem.at[i])
        for i, (h, v) in enumerate(((wg_hbm, wg), (wu_hbm, wu), (wd_hbm, wd)))
    ]
    for ld in loads:
        ld.start()

    barrier = pltpu.get_barrier_semaphore()
    peers = [right, left, mate1, mate2]
    for s in range(1, slots):
        peers.append(dev(y, z, *slot_dest(s)))
    for peer in peers:
        pl.semaphore_signal(barrier, inc=1, device_id=peer, device_id_type=MESH)
    pl.semaphore_wait(barrier, len(peers))

    def remote(src, dst, ssem, rsem, device):
        return pltpu.make_async_remote_copy(
            src_ref=src, dst_ref=dst, send_sem=ssem, recv_sem=rsem,
            device_id=device, device_id_type=MESH,
        )

    pieces = ((0, tb // 2), (tb // 2, tb // 2 + 2 * top))

    def z_hops(to_right, piece):
        return far if to_right == (piece == 0) else far - 1

    def z_copy(to_right, h, piece):
        sign = -1 if to_right else 1

        def at(hops):
            return entry[far if hops == far else sign * hops]

        rows = pl.ds(*pieces[piece])
        source = tok_ref.at[rows] if (h == 1 and piece == 0) else tokg.at[at(h - 1), rows]
        d = 0 if to_right else 1
        return remote(
            source, tokg.at[at(h), rows], z_ssem.at[d, piece, h - 1], z_rsem.at[d, piece, h - 1],
            right if to_right else left,
        )

    def z_start(h, piece):
        for to_right in (True, False):
            if h <= z_hops(to_right, piece):
                z_copy(to_right, h, piece).start()

    def relay(h, piece):
        for to_right in (True, False):
            if h <= z_hops(to_right, piece):
                z_copy(to_right, h, piece).wait_recv()
                if h < z_hops(to_right, piece):
                    z_copy(to_right, h + 1, piece).start()

    z_start(1, 0)

    def iota(shape, dim):
        return lax.broadcasted_iota(I32, shape, dim)

    def column(row):
        n = row.shape[1]
        return jnp.sum(jnp.where(iota((n, n), 0) == iota((n, n), 1), row, 0), axis=1, keepdims=True)

    reps = experts + hot
    hot_col = column(place_ref[0:1, :])
    host_col = column(place_ref[1:2, :])
    cap_col = column(cap_ref[...])
    r_iota = iota((reps, tb), 0)
    j_iota = iota((hot, tb), 0)
    targets = []
    chosen = jnp.zeros((reps, tb), F32)
    for k in range(top):
        idk = ids_ref[k : k + 1, :]
        j = jnp.sum(jnp.where(hot_col == idk, j_iota, 0), axis=0, keepdims=True)
        t = jnp.where(rep_ref[k : k + 1, :] == 1, experts + j, idk)
        targets.append(t)
        chosen = chosen + jnp.where(r_iota == t, 1.0, 0.0)
    earlier = jnp.where(iota((tb, tb), 0) < iota((tb, tb), 1), 1.0, 0.0).astype(BF16)
    rank = jnp.dot(chosen.astype(BF16), earlier, preferred_element_type=F32).astype(I32)
    own_code = r_iota[:experts] * CODE + rank[:experts]
    rank_c = rank[experts:]
    copy_code = jnp.where(
        rank_c < half,
        hot_col * CODE + cap + rank_c,
        host_col * CODE + (cap - half) + rank_c,
    )
    code = jnp.concatenate([own_code, copy_code], axis=0)
    code = jnp.where(rank < cap_col, code, -CODE)
    rows = [
        jnp.sum(jnp.where(r_iota == targets[k], code, 0), axis=0, keepdims=True) for k in range(top)
    ]
    code = jnp.concatenate(rows, axis=0)
    whose = jnp.right_shift(code, 6)
    gw = gw_ref[...]
    gw_hi = gw.astype(BF16)
    gw_lo = (gw - gw_hi.astype(F32)).astype(BF16)
    tail = (whose.astype(F32).astype(BF16), (code - whose * CODE).astype(F32).astype(BF16), gw_hi, gw_lo)
    tokg[0, tb:] = jnp.zeros((2 * top, cols), BF16)
    for i, t in enumerate(tail):
        tokg[0, tb : tb + top, i * tb : (i + 1) * tb] = t
    tokg[0, :tb] = tok_ref[...]
    z_start(1, 1)

    role = jnp.int32(0)
    for j in range(hot):
        role = jnp.maximum(role, jnp.where(place_s[1, j] == e, 1, 0))

    def read_codes(n):
        t = tokg[n, tb : tb + top, 0 : 4 * tb].astype(F32)
        codes[n, 0] = t[:, :tb] * CODE + t[:, tb : 2 * tb]
        codes[n, 1] = t[:, 2 * tb : 3 * tb]
        codes[n, 2] = t[:, 3 * tb :]

    def layout(rr, blocks):
        p = iota((rr, 1), 0)
        block_of = jnp.zeros((rr, 1), I32)
        for i in range(1, blocks + 1):
            block_of = block_of + jnp.where(p >= i * each, 1, 0)
        return block_of, p - block_of * each

    def slot_keys(rr, blocks, i, source):
        block_of, local = layout(rr, blocks)
        keys = []
        for s in range(slots):
            xx, cc = slot_dest(s)
            key = ((z * nx + xx) * nc + cc) * CODE + local
            keys.append(jnp.where(block_of == i, key, -2))
        return jnp.concatenate(keys, axis=0).astype(F32)

    def x_copy(g, s):
        xx, cc = slot_dest(s)
        return remote(xs[g].at[s], xr[g].at[s], x_ssem.at[g, s], x_rsem.at[g, s], dev(y, z, xx, cc))

    def loop(lo, hi, f):
        def body(i, carry):
            f(i)
            return carry

        lax.fori_loop(lo, hi, body, 0)

    def dispatch(g):
        blocks = groups[g]
        nb = len(blocks)
        rr = room(cfg, nb)
        n0 = entry[blocks[0]]
        sel = []
        for i in range(nb):
            read_codes(n0 + i)
            keys = slot_keys(rr, nb, i, False)
            hit = jnp.zeros((slots * rr, tb), jnp.bool_)
            for k in range(top):
                hit = hit | (codes[n0 + i, 0, k : k + 1, :] == keys)
            sel.append(jnp.where(hit, 1.0, 0.0).astype(BF16))
        sel = jnp.concatenate(sel, axis=1)
        toks = tokg[n0 : n0 + nb, :tb].reshape(nb * tb, cols)
        picked = jnp.dot(sel, toks, preferred_element_type=F32)
        xs[g][...] = picked.reshape(slots, rr, cols).astype(BF16)
        loop(1, slots, lambda s: x_copy(g, s).start())
        xr[g][0] = picked[0:rr].astype(BF16)

    def joined(ref):
        return ref[...].astype(F32).reshape(slots * ref.shape[1], cols).astype(BF16)

    def unit_rows(rr, i):
        p = iota((ur, 1), 0)
        s = jnp.zeros((ur, 1), I32)
        for j in range(1, slots):
            s = s + jnp.where(p >= j * cap, 1, 0) * jnp.where(p < ua, 1, 0)
            s = s + jnp.where(p >= ua + j * half, 1, 0)
        local = jnp.where(p < ua, p - s * cap, p - ua - s * half + cap)
        return s * rr + i * each + local

    def arrive(g):
        blocks = groups[g]
        rr = room(cfg, len(blocks))
        loop(1, slots, lambda s: x_copy(g, s).wait_recv())
        rows = joined(xr[g])
        for i, b in enumerate(blocks):
            perm = jnp.where(unit_rows(rr, i) == iota((ur, slots * rr), 1), 1.0, 0.0).astype(BF16)
            xc[place_of[b]] = jnp.dot(perm, rows, preferred_element_type=F32).astype(BF16)

    def y_copy(stage, u, ab):
        if stage == 0:
            return remote(r1s.at[u, ab], r1r.at[u, ab], r1_ssem.at[u, ab], r1_rsem.at[u, ab], first_mate[ab])
        if stage == 1:
            return remote(r2s.at[u, ab], r2r.at[u, ab], r2_ssem.at[u, ab], r2_rsem.at[u, ab], second_mate[ab])
        if stage == 2:
            ref = hid.at[u, pl.ds(4 * ab + 2 * keep_half[ab] + keep_quarter[ab], 1)]
            return remote(ref, ref, a1_ssem.at[u, ab], a1_rsem.at[u, ab], second_mate[ab])
        ref = hid.at[u, pl.ds(4 * ab + 2 * keep_half[ab], 2)]
        return remote(ref, ref, a2_ssem.at[u, ab], a2_rsem.at[u, ab], first_mate[ab])

    def y_recv(stage, u, ab):
        if stage < 2:
            y_copy(stage, u, ab).wait_recv()
        elif stage == 2:
            ref = hid.at[u, pl.ds(4 * ab + 2 * keep_half[ab] + 1 - keep_quarter[ab], 1)]
            remote(ref, ref, a1_ssem.at[u, ab], a1_rsem.at[u, ab], second_mate[ab]).wait_recv()
        else:
            ref = hid.at[u, pl.ds(4 * ab + 2 * (1 - keep_half[ab]), 2)]
            remote(ref, ref, a2_ssem.at[u, ab], a2_rsem.at[u, ab], first_mate[ab]).wait_recv()

    def stage_up(u):
        def block(b):
            at = pl.ds(pl.multiple_of(b * LANES, LANES), LANES)
            wa = jnp.concatenate([wg[0, :, at], wu[0, :, at]], axis=1)
            wb = jnp.concatenate([wg[role, :, at], wu[role, :, at]], axis=1)
            ya = jnp.dot(xc[u, :ua], wa, preferred_element_type=F32)
            yb = jnp.dot(xc[u, ua:], wb, preferred_element_type=F32)
            return jnp.concatenate([ya, yb], axis=0)

        for ab in range(2):

            def send(j, ab=ab):
                r1s[u, ab, j] = block(4 * ab + 2 * (1 - keep_half[ab]) + j).astype(BF16)

            loop(0, 2, send)
            y_copy(0, u, ab).start()
        for ab in range(2):

            def keep(j, ab=ab):
                part[u, ab, j] = block(4 * ab + 2 * keep_half[ab] + j)

            loop(0, 2, keep)

    def stage_sum(u):
        for ab in range(2):
            y_recv(0, u, ab)
            mine, other = keep_quarter[ab], 1 - keep_quarter[ab]
            r2s[u, ab] = (part[u, ab, other] + r1r[u, ab, other].astype(F32)).astype(BF16)
            y_copy(1, u, ab).start()
            part[u, ab, mine] = part[u, ab, mine] + r1r[u, ab, mine].astype(F32)

    def stage_act(u):
        for ab in range(2):
            y_recv(1, u, ab)
            v = part[u, ab, keep_quarter[ab]] + r2r[u, ab].astype(F32)
            gate, up = v[:, :LANES], v[:, LANES:]
            hidden = gate / (1.0 + jnp.exp(-gate)) * up
            hid[u, 4 * ab + 2 * keep_half[ab] + keep_quarter[ab]] = hidden.astype(BF16)
            y_copy(2, u, ab).start()

    def stage_pass(u):
        for ab in range(2):
            y_recv(2, u, ab)
            y_copy(3, u, ab).start()

    def stage_down(u):
        for ab in range(2):
            y_recv(3, u, ab)
        h = jnp.concatenate([hid[u, b] for b in range(8)], axis=1)
        res[u, :ua] = jnp.dot(h[:ua], wd[0], preferred_element_type=F32).astype(BF16)
        res[u, ua:] = jnp.dot(h[ua:], wd[role], preferred_element_type=F32).astype(BF16)

    def o_copy(r, s):
        xx, cc = slot_source(s)
        return remote(os_[r].at[s], or_[r].at[s], o_ssem.at[r, s], o_rsem.at[r, s], dev(y, z, xx, cc))

    def give_back(r):
        blocks = returns[r]
        nb = len(blocks)
        rr = room(cfg, nb)
        u0 = place_of[blocks[0]]
        block_of, local = layout(rr, nb)
        home = []
        for s in range(slots):
            at = jnp.where(local < cap, s * cap + local, ua + s * half + local - cap) + block_of * ur
            home.append(jnp.where(block_of < nb, at, -1))
        home = jnp.concatenate(home, axis=0)
        perm = jnp.where(home == iota((slots * rr, nb * ur), 1), 1.0, 0.0).astype(BF16)
        rows = res[u0 : u0 + nb].reshape(nb * ur, cols)
        spread = jnp.dot(perm, rows, preferred_element_type=F32)
        os_[r][...] = spread.reshape(slots, rr, cols).astype(BF16)
        loop(1, slots, lambda s: o_copy(r, s).start())
        or_[r][0] = spread[0:rr].astype(BF16)

    def combine(r):
        blocks = returns[r]
        nb = len(blocks)
        rr = room(cfg, nb)
        loop(1, slots, lambda s: o_copy(r, s).wait_recv())
        rows = joined(or_[r])
        for i, b in enumerate(blocks):
            n = entry[b]
            keys = slot_keys(rr, nb, i, True)
            w_hi = jnp.zeros((slots * rr, tb), F32)
            w_lo = jnp.zeros((slots * rr, tb), F32)
            for k in range(top):
                hit = codes[n, 0, k : k + 1, :] == keys
                w_hi = jnp.where(hit, codes[n, 1, k : k + 1, :], w_hi)
                w_lo = jnp.where(hit, codes[n, 2, k : k + 1, :], w_lo)
            dims = (((0,), (0,)), ((), ()))
            total = lax.dot_general(w_hi.astype(BF16), rows, dims, preferred_element_type=F32)
            acc[n] = total + lax.dot_general(w_lo.astype(BF16), rows, dims, preferred_element_type=F32)

    def c_copy(to_right, h, part_):
        i = (h - 1) if to_right else far + (h - 1)
        at = pl.ds(part_ * (tb // 2), tb // 2)
        return remote(
            csend.at[i, at], crecv.at[i, at], c_ssem.at[i, part_], c_rsem.at[i, part_],
            right if to_right else left,
        )

    def c_hop(to_right, h):
        d = (far - h + 1) if to_right else h - far
        i = (h - 1) if to_right else far + (h - 1)
        for part_ in range(2):
            at = slice(part_ * (tb // 2), (part_ + 1) * (tb // 2))
            v = acc[entry[d], at]
            if h > 1:
                c_copy(to_right, h - 1, part_).wait_recv()
                v = v + crecv[i - 1, at].astype(F32)
            csend[i, at] = v.astype(BF16)
            c_copy(to_right, h, part_).start()

    words = {
        "d": dispatch, "a": arrive, "u": stage_up, "s": stage_sum, "c": stage_act, "p": stage_pass, "e": stage_down,
        "o": give_back, "m": combine,
        "R": lambda h: c_hop(True, h), "L": lambda h: c_hop(False, h),
    }

    def run(text):
        for word in text.split():
            if word[0] == "r":
                relay(int(word[1]), int(word[2]))
            elif word[0] == "w":
                for ld in loads:
                    ld.wait()
            else:
                words[word[0]](int(word[1:]))

    for text in cfg["early"]:
        run(text)

    def step(n):
        for k, text in cfg["before"].items():

            @pl.when(n == k)
            def _(text=text):
                run(text)

        for lag, stage in enumerate((stage_up, stage_sum, stage_act, stage_pass, stage_down)):
            u = n - lag

            @pl.when((u >= cfg["begin"][lag]) & (u < units))
            def _(stage=stage, u=u):
                stage(u)

        for k, text in cfg["after"].items():

            @pl.when(n == k)
            def _(text=text):
                run(text)

    loop(cfg["begin"][0], units + 4, step)
    for text in cfg["late"]:
        run(text)
    for part_ in range(2):
        at = slice(part_ * (tb // 2), (part_ + 1) * (tb // 2))
        c_copy(True, far, part_).wait_recv()
        c_copy(False, far - 1, part_).wait_recv()
        v = acc[0, at] + crecv[far - 1, at].astype(F32) + crecv[nz - 2, at].astype(F32)
        out_ref[at, :] = v.astype(BF16)

    for to_right in (True, False):
        for piece in range(2):
            for h in range(1, z_hops(to_right, piece) + 1):
                z_copy(to_right, h, piece).wait_send()
            for h in range(1, (far if to_right else far - 1) + 1):
                c_copy(to_right, h, piece).wait_send()
    for g in range(ng):
        loop(1, slots, lambda s, g=g: x_copy(g, s).wait_send())
    for r in range(nr):
        loop(1, slots, lambda s, r=r: o_copy(r, s).wait_send())

    def sent_y(u):
        for ab in range(2):
            for stage in range(4):
                y_copy(stage, u, ab).wait_send()

    loop(0, units, sent_y)


def on_device(
    cfg, tokens, expert_ids, replica_choice, gate_weights, placement, capacity, w_gate, w_up, w_down
):
    nz, nx, nc, cap = cfg["nz"], cfg["nx"], cfg["nc"], cfg["cap"]
    groups, returns = cfg["groups"], cfg["returns"]
    tb, cols = tokens.shape
    top = expert_ids.shape[1]
    ff = w_gate.shape[-1]
    slots = nx * nc
    ur = slots * (cap + cap // 2)
    far = nz // 2
    units = nz
    vmem = pl.BlockSpec(memory_space=pltpu.VMEM)
    smem = pl.BlockSpec(memory_space=pltpu.SMEM)
    anywhere = pl.BlockSpec(memory_space=pl.ANY)
    dma = pltpu.SemaphoreType.DMA
    assert ff == 8 * LANES and top == 8

    def buf(*shape):
        return pltpu.VMEM(shape, BF16)

    scratch = [buf(2, cols, ff), buf(2, cols, ff), buf(2, ff, cols), dma((3,))]
    scratch += [buf(nz, tb + 2 * top, cols), pltpu.VMEM((nz, 3, top, tb), F32), dma((2, 2, far)), dma((2, 2, far))]
    scratch += [buf(slots, room(cfg, len(g)), cols) for _ in range(2) for g in groups]
    scratch += [dma((len(groups), slots)), dma((len(groups), slots)), buf(units, ur, cols)]
    scratch += [
        pltpu.VMEM((units, 2, 2, ur, 2 * LANES), F32),
        buf(units, 2, 2, ur, 2 * LANES), buf(units, 2, 2, ur, 2 * LANES),
        buf(units, 2, ur, 2 * LANES), buf(units, 2, ur, 2 * LANES),
        buf(units, 8, ur, LANES), buf(units, ur, cols),
    ]
    scratch += [dma((units, 2)) for _ in range(8)]
    scratch += [buf(slots, room(cfg, len(r)), cols) for _ in range(2) for r in returns]
    scratch += [dma((len(returns), slots)), dma((len(returns), slots))]
    scratch += [
        pltpu.VMEM((nz, tb, cols), F32), buf(nz - 1, tb, cols), buf(nz - 1, tb, cols),
        dma((nz - 1, 2)), dma((nz - 1, 2)),
    ]
    return pl.pallas_call(
        functools.partial(kernel, cfg),
        out_shape=jax.ShapeDtypeStruct((tb, cols), BF16),
        in_specs=[vmem, vmem, vmem, vmem, vmem, smem, vmem, anywhere, anywhere, anywhere],
        out_specs=vmem,
        scratch_shapes=scratch,
        compiler_params=pltpu.CompilerParams(
            collective_id=0, has_side_effects=True, vmem_limit_bytes=60 * 2**20
        ),
    )(
        tokens, expert_ids.T, replica_choice.T, gate_weights.T, placement.T, placement.T,
        capacity.reshape(1, -1), w_gate, w_up, w_down,
    )


def solution(mesh, cfg=None):
    return jax.shard_map(
        functools.partial(on_device, cfg or SIZES),
        mesh=mesh,
        in_specs=(
            P("expert", "dp"),
            P("expert", None),
            P("expert", None),
            P("expert", None),
            P(),
            P(),
            P("expert", None, "dp", None),
            P("expert", None, "dp", None),
            P("expert", None, None, "dp"),
        ),
        out_specs=P("expert", "dp"),
        check_vma=False,
    )
```

profile of v0, /device:TPU:2, one launch (start us, length us, event | category | flops | bytes accessed | tf_op | source)
XLA Modules:
  0.0 120.3 jit_solution(11116805716228206705)
XLA Ops:
  0.0 118.6 %shard_map.91 = bf16[128,896]{1,0:T(8,128)(2,1)} custom-call(bf16[128,896]{1,0:T(8,128)(2,1)} %refs_0_.1, s32[8,128]{1,0:T(8,128)} %bitcast.5, s32[8,128]{1,0:T(8,128)} %bitcast.6, f32[8,128]{1,0:T(8,128)} %bitcast.7, s32[2,32]{1,0:T(2,128)} %bitcast.8, s32[2,32]{1,0:T(2,128)} %bitcast.9, s32[1,96]{1,0:T(1,128)} %bitcast.10, ...), custom_call_target="tpu_custom_call" | custom-call | tf_op jit(solution)/shard_map/pallas_call | solution.py:522
  118.6 1.6 %copy.11 = bf16[128,896]{1,0:T(8,128)(2,1)} copy(bf16[128,896]{1,0:T(8,128)(2,1)} %shard_map.91) | data formatting | bytes 458752
where the time goes:
time: 120 us
  Pallas kernels  119 us (99%)
  local copies, waits for them, and re-layouts  1.65 us (1%)
    pallas_call x1, Pallas kernels, on_device(): pl.pallas_call(functools.partial(kernel, cfg), out_shape=jax.ShapeDtypeSt...  119 us

commit v1 on v0

--- a/solution.py
+++ b/solution.py
@@ -113,7 +113,6 @@
         peers.append(dev(y, z, *slot_dest(s)))
     for peer in peers:
         pl.semaphore_signal(barrier, inc=1, device_id=peer, device_id_type=MESH)
-    pl.semaphore_wait(barrier, len(peers))
 
     def remote(src, dst, ssem, rsem, device):
         return pltpu.make_async_remote_copy(
@@ -152,7 +151,6 @@
                 if h < z_hops(to_right, piece):
                     z_copy(to_right, h + 1, piece).start()
 
-    z_start(1, 0)
 
     def iota(shape, dim):
         return lax.broadcasted_iota(I32, shape, dim)
@@ -199,6 +197,8 @@
     for i, t in enumerate(tail):
         tokg[0, tb : tb + top, i * tb : (i + 1) * tb] = t
     tokg[0, :tb] = tok_ref[...]
+    pl.semaphore_wait(barrier, len(peers))
+    z_start(1, 0)
     z_start(1, 1)
 
     role = jnp.int32(0)

time: 120 us -> 121 us (level)
  no operation moved by 1% of the time
where the time goes in v1:
time: 121 us
  Pallas kernels  119 us (98%)
  local copies, waits for them, and re-layouts  1.65 us (1%)
    pallas_call x1, Pallas kernels, on_device(): pl.pallas_call(functools.partial(kernel, cfg), out_shape=jax.ShapeDtypeSt...  119 us

profile of v1, /device:TPU:2, one launch (start us, length us, event | category | flops | bytes accessed | tf_op | source)
XLA Modules:
  0.0 120.6 jit_solution(4019526188592565428)
XLA Ops:
  0.0 118.9 %shard_map.91 = bf16[128,896]{1,0:T(8,128)(2,1)} custom-call(bf16[128,896]{1,0:T(8,128)(2,1)} %refs_0_.1, s32[8,128]{1,0:T(8,128)} %bitcast.5, s32[8,128]{1,0:T(8,128)} %bitcast.6, f32[8,128]{1,0:T(8,128)} %bitcast.7, s32[2,32]{1,0:T(2,128)} %bitcast.8, s32[2,32]{1,0:T(2,128)} %bitcast.9, s32[1,96]{1,0:T(1,128)} %bitcast.10, ...), custom_call_target="tpu_custom_call" | custom-call | tf_op jit(solution)/shard_map/pallas_call | solution.py:522
  118.9 1.6 %copy.11 = bf16[128,896]{1,0:T(8,128)(2,1)} copy(bf16[128,896]{1,0:T(8,128)(2,1)} %shard_map.91) | data formatting | bytes 458752
